TPU v7x, 512 devices: a whole 4x4x16 slice. The times are simulated.
512 devices in a mesh: gx: 8 (over z_lo), gy: 4 (over z_hi, core), gz: 16 (over y, x).
Axes of the slice: x: 4, y: 4, z: 16 (z_hi: 2, z_lo: 8; z = z_hi * 8 + z_lo), core: 2. Of those that a mesh axis runs over, the one named last changes fastest.
Arguments:
- probe_vectors: float32 [32, 16, 32, 2048], P(None, 'gx', 'gy', 'gz'), may hold values from -6 to 6
- layer_ids: int32 [16, 32, 2048], P('gx', 'gy', 'gz'), may hold values from 0 to 15
- layer_kappa: float32 [16], replicated, may hold values from 0.1 to 10
- slot_order: int32 [32, 16], replicated, may hold values from 0 to 511, as said below
Outputs:
- factored: float32 [16384, 16384], P(('gx', 'gy'), 'gz')
Inputs may be any that keep to these rules, and one draw needn't show every extreme that they name: `slot_order`: the entries are an ordering of 0 to 511, and in each column the entries divided by 16, rounded down, are an ordering of 0 to 31.
All inputs are finite; a program needn't handle non-finite values.
Results may differ from a plain program's by a relative error of at most 0.00013.
Values sent between devices are 32-bit elements; how exact they have to be, the bound alone decides.
No kernel may reach another device: no remote copies, remote signals or barrier semaphores. Data moves between devices by JAX's collectives and lax.ppermute only.
A program may use at most 128 MiB of HBM per device.

v0:
```python
import math
import jax
import jax.numpy as jnp
from jax import lax
from jax.sharding import PartitionSpec as P

PASSES = 4
PANEL = 256
NPAN = 2
upper_edge = 120.0
lower_edge = 24.0
coarse_shift = 1.0


def with_halo(block, sides, width):
    for axis, dim in sides:
        count = lax.axis_size(axis)
        forward = [(i, i + 1) for i in range(count - 1)]
        backward = [(target, source) for source, target in forward]
        low = lax.ppermute(
            lax.slice_in_dim(block, block.shape[dim] - width, None, axis=dim), axis, forward
        )
        high = lax.ppermute(lax.slice_in_dim(block, 0, width, axis=dim), axis, backward)
        block = jnp.concatenate([low, block, high], axis=dim)
    return block


def from_root(value, axis, source):
    kept = jnp.where(lax.axis_index(axis) == source, value, 0).astype(value.dtype)
    return lax.psum(kept, axis)


def cheb_factors(step_index):
    center = (upper_edge + lower_edge) / (upper_edge - lower_edge)
    growth = math.log(center + math.sqrt(center * center - 1.0))

    def chebval(degree):
        expo = math.exp(degree * growth)
        return 0.5 * (expo + 1.0 / expo)

    if step_index == 0:
        return (1.0 / chebval(1), 0.0)
    return (
        2.0 * chebval(step_index) / chebval(step_index + 1),
        chebval(step_index - 1) / chebval(step_index + 1),
    )


def face_weights(kappa_pad):
    center = kappa_pad[1:-1, 1:-1, 1:-1]
    x_plus = 0.5 * (center + kappa_pad[2:, 1:-1, 1:-1])
    x_minus = 0.5 * (center + kappa_pad[:-2, 1:-1, 1:-1])
    y_plus = 0.5 * (center + kappa_pad[1:-1, 2:, 1:-1])
    y_minus = 0.5 * (center + kappa_pad[1:-1, :-2, 1:-1])
    z_plus = 0.5 * (center + kappa_pad[1:-1, 1:-1, 2:])
    z_minus = 0.5 * (center + kappa_pad[1:-1, 1:-1, :-2])
    diagonal = x_plus + x_minus + y_plus + y_minus + z_plus + z_minus
    return ((x_plus, x_minus, y_plus, y_minus, z_plus, z_minus), diagonal)


def apply_operator(field_pad, weights, diagonal):
    x_plus, x_minus, y_plus, y_minus, z_plus, z_minus = weights
    interior = field_pad[..., 1:-1, 1:-1, 1:-1]
    beside = x_plus * field_pad[..., 2:, 1:-1, 1:-1] + x_minus * field_pad[..., :-2, 1:-1, 1:-1]
    beside = (
        beside + y_plus * field_pad[..., 1:-1, 2:, 1:-1] + y_minus * field_pad[..., 1:-1, :-2, 1:-1]
    )
    beside = (
        beside + z_plus * field_pad[..., 1:-1, 1:-1, 2:] + z_minus * field_pad[..., 1:-1, 1:-1, :-2]
    )
    return diagonal * interior - beside


def cheb_update(current, previous, applied, step_index):
    factor_one, factor_two = cheb_factors(step_index)
    shifted = (upper_edge + lower_edge) / (upper_edge - lower_edge) * current - 2.0 / (
        upper_edge - lower_edge
    ) * applied
    return factor_one * shifted - factor_two * previous


def face_block(own_face, weight_face, ghost_face, scaling):
    return -scaling * jnp.einsum(
        "kab,ab,lab->kl", own_face, weight_face, ghost_face, precision=lax.Precision.HIGHEST
    )


def table_lookup(table, row_wanted, col_wanted):
    row_ids = jnp.arange(table.shape[0], dtype=jnp.int32)
    col_ids = jnp.arange(table.shape[1], dtype=jnp.int32)
    hit = (row_wanted[..., None, None] == row_ids[:, None]) & (
        col_wanted[..., None, None] == col_ids[None, :]
    )
    return jnp.sum(jnp.where(hit, table, 0), axis=(-2, -1))


def on_device(probe_vectors, layer_ids, layer_kappa, slot_order):
    highest = lax.Precision.HIGHEST
    grid_x = lax.axis_size("gx")
    grid_y = lax.axis_size("gy")
    grid_z = lax.axis_size("gz")
    index_x = lax.axis_index("gx")
    index_y = lax.axis_index("gy")
    index_z = lax.axis_index("gz")
    vectors, extent_x, extent_y, extent_z = probe_vectors.shape
    layers = layer_kappa.shape[0]
    choose = layer_ids[None] == jnp.arange(layers, dtype=jnp.int32)[:, None, None, None]
    conductivity = jnp.sum(jnp.where(choose, layer_kappa[:, None, None, None], 0.0), axis=0)
    kappa_pad = with_halo(conductivity, (("gx", 0), ("gy", 1), ("gz", 2)), 1)
    weights, diagonal = face_weights(kappa_pad)
    current = probe_vectors
    previous = jnp.zeros_like(probe_vectors)
    for step_index in range(PASSES):
        padded = with_halo(current, (("gx", 1), ("gy", 2), ("gz", 3)), 1)
        applied = apply_operator(padded, weights, diagonal)
        current, previous = (cheb_update(current, previous, applied, step_index), current)
    ghosts = with_halo(current, (("gx", 1), ("gy", 2), ("gz", 3)), 1)
    local_image = apply_operator(
        jnp.pad(current, ((0, 0), (1, 1), (1, 1), (1, 1))), weights, diagonal
    )
    cell_count = extent_x * extent_y * extent_z
    scaling = 1.0 / math.sqrt(cell_count)
    flattened = current.reshape(vectors, cell_count)
    own_block = scaling * jnp.dot(
        flattened, local_image.reshape(vectors, cell_count).T, precision=highest
    )
    own_block = own_block + coarse_shift * jnp.eye(vectors, dtype=jnp.float32)
    x_plus, x_minus, y_plus, y_minus, z_plus, z_minus = weights
    blocks = jnp.stack(
        [
            own_block,
            face_block(current[:, 0], x_minus[0], ghosts[:, 0, 1:-1, 1:-1], scaling),
            face_block(current[:, -1], x_plus[-1], ghosts[:, -1, 1:-1, 1:-1], scaling),
            face_block(current[:, :, 0], y_minus[:, 0], ghosts[:, 1:-1, 0, 1:-1], scaling),
            face_block(current[:, :, -1], y_plus[:, -1], ghosts[:, 1:-1, -1, 1:-1], scaling),
            face_block(current[:, :, :, 0], z_minus[:, :, 0], ghosts[:, 1:-1, 1:-1, 0], scaling),
            face_block(current[:, :, :, -1], z_plus[:, :, -1], ghosts[:, 1:-1, 1:-1, -1], scaling),
        ]
    )
    rows_total = grid_x * grid_y
    row_index = index_x * grid_y + index_y
    row_ids = jnp.arange(rows_total, dtype=jnp.int32)
    group_of = slot_order // grid_z
    column_groups = lax.dynamic_index_in_dim(group_of, index_z, 1, keepdims=False)
    owner_source = jnp.sum(jnp.where(column_groups == row_index, row_ids, 0))
    piece = lax.all_gather(blocks[None], ("gx", "gy"), axis=0, tiled=True)
    anchor = jnp.arange(piece.shape[0], dtype=jnp.int32)
    wanted = (anchor == owner_source)[:, None, None, None]
    owned = jnp.sum(jnp.where(wanted, piece, 0.0), axis=0)
    sources = jnp.arange(grid_z, dtype=jnp.int32)
    source_rows = jnp.sum(jnp.where(group_of == row_index, row_ids[:, None], 0), axis=0)
    source_x = source_rows // grid_y
    source_y = source_rows % grid_y
    neighbour_rows = jnp.stack(
        [
            source_rows,
            source_rows - grid_y,
            source_rows + grid_y,
            source_rows - 1,
            source_rows + 1,
            source_rows,
            source_rows,
        ],
        axis=1,
    )
    neighbour_cols = jnp.stack(
        [sources, sources, sources, sources, sources, sources - 1, sources + 1], axis=1
    )
    always = jnp.ones((grid_z,), bool)
    usable = jnp.stack(
        [
            always,
            source_x > 0,
            source_x < grid_x - 1,
            source_y > 0,
            source_y < grid_y - 1,
            sources > 0,
            sources < grid_z - 1,
        ],
        axis=1,
    )
    targets = table_lookup(slot_order, neighbour_rows, neighbour_cols)
    own_slots = table_lookup(slot_order, source_rows, sources) - row_index * grid_z
    local_cols = targets - index_z * rows_total
    usable = usable & (local_cols >= 0) & (local_cols < rows_total)
    col_flat = jnp.where(usable, local_cols, rows_total).reshape(-1)
    row_flat = jnp.broadcast_to(own_slots[:, None], (grid_z, 7)).reshape(-1)
    empty_grid = jnp.zeros((grid_z, vectors, rows_total, vectors), jnp.float32)
    gathered = empty_grid.at[row_flat, :, col_flat, :].add(
        lax.all_gather(owned, "gz", axis=0, tiled=True), mode="drop"
    )
    coarse = gathered.reshape(grid_z * vectors, rows_total * vectors)
    rows_local = coarse.shape[0]
    cols_local = coarse.shape[1]
    panel_width = min(PANEL, rows_local, cols_local)
    global_rows = row_index * rows_local + jnp.arange(rows_local, dtype=jnp.int32)
    global_cols = index_z * cols_local + jnp.arange(cols_local, dtype=jnp.int32)
    offsets = jnp.arange(panel_width, dtype=jnp.int32)
    for panel_index in range(NPAN):
        panel_begin = panel_index * panel_width
        panel_end = panel_begin + panel_width
        row_root = panel_begin // rows_local
        col_root = panel_begin // cols_local
        row_start = panel_begin - row_root * rows_local
        col_start = panel_begin - col_root * cols_local
        column_piece = from_root(coarse[:, col_start : col_start + panel_width], "gz", col_root)
        row_piece, diagonal_piece = (
            from_root(coarse[row_start : row_start + panel_width, :], ("gx", "gy"), row_root),
            from_root(column_piece[row_start : row_start + panel_width, :], ("gx", "gy"), row_root),
        )
        factor = jnp.linalg.cholesky(diagonal_piece)
        row_factor = jax.scipy.linalg.solve_triangular(factor, column_piece.T, lower=True).T
        col_factor = jax.scipy.linalg.solve_triangular(factor, row_piece, lower=True).T
        row_factor = jnp.where(
            global_rows[:, None] >= panel_begin + offsets[None, :], row_factor, 0.0
        )
        updated = coarse - jnp.dot(row_factor, col_factor.T, precision=highest)
        trail_rows = global_rows >= panel_end
        trail_cols = global_cols >= panel_end
        panel_rows = (global_rows >= panel_begin) & (global_rows < panel_end)
        coarse = jnp.where(
            trail_rows[:, None] & trail_cols[None, :],
            updated,
            jnp.where(panel_rows[:, None] & trail_cols[None, :], 0.0, coarse),
        )
        old_columns = coarse[:, col_start : col_start + panel_width]
        new_columns = jnp.where(index_z == col_root, row_factor, old_columns)
        coarse = coarse.at[:, col_start : col_start + panel_width].set(new_columns)
    return coarse


def solution(mesh):
    in_specs = (P(None, "gx", "gy", "gz"), P("gx", "gy", "gz"), P(), P())
    out_specs = P(("gx", "gy"), "gz")
    return jax.shard_map(
        on_device, mesh=mesh, in_specs=in_specs, out_specs=out_specs, check_vma=False
    )
```

profile of v0, /device:TPU:1, one launch (start us, length us, event | category | flops | bytes accessed | tf_op | source)
XLA Modules:
  0.0 1363.8 jit_solution(13902177501467770364)
XLA Ops:
  8.7 5.0 collective-permute-start.1
  14.7 3.6 collective-permute-start.7
  20.8 3.0 select_reduce_fusion.1
  23.9 15.8 %collective-permute-start.3 = (f32[4,1,128]{2,1,0:T(1,128)S(1)}, f32[4,1,128]{2,1,0:T(1,128)S(1)}, u32[]{:S(2)}, u32[]{:S(2)}) collective-permute-start(f32[4,1,128]{2,1,0:T(1,128)S(1)} %get-tuple-element.143), channel_id=1, source_target_pairs={{0,16},{16,32},{32,48},{1,17},{17,33},{33,49},{2,18},{18,34},{34,5... | collective-permute-start | bytes 6152 | tf_op jit(solution)/shard_map/ppermute | solution.py:20
  41.7 11.6 collective-permute-done.2
  54.7 4.0 collective-permute-start.5
  62.7 12.4 collective-permute-start.9
  78.7 4.3 collective-permute-start.11
  85.8 4.8 collective-permute-start.13
  94.5 14.7 %collective-permute-start.15 = (f32[32,4,1,128]{3,0,2,1:T(8,128)S(1)}, f32[32,4,1,128]{3,0,2,1:T(8,128)S(1)}, u32[]{:S(2)}, u32[]{:S(2)}) collective-permute-start(f32[32,4,1,128]{3,0,2,1:T(8,128)S(1)} %get-tuple-element.117), channel_id=1, source_target_pairs={{0,16},{16,32},{32,48},{1,17},{17,33},{33,49},{2,18},{18,34},{34,5... | collective-permute-start | bytes 196616 | tf_op jit(solution)/shard_map/ppermute | solution.py:20
  113.1 4.6 collective-permute-start.17
  121.1 5.0 collective-permute-start.19
  130.0 14.2 %collective-permute-start.21 = (f32[32,4,1,128]{3,0,2,1:T(8,128)S(1)}, f32[32,4,1,128]{3,0,2,1:T(8,128)S(1)}, u32[]{:S(2)}, u32[]{:S(2)}) collective-permute-start(f32[32,4,1,128]{3,0,2,1:T(8,128)S(1)} %get-tuple-element.115), channel_id=1, source_target_pairs={{0,16},{16,32},{32,48},{1,17},{17,33},{33,49},{2,18},{18,34},{34,5... | collective-permute-start | bytes 196616 | tf_op jit(solution)/shard_map/ppermute | solution.py:20
  147.7 4.5 collective-permute-start.23
  155.2 4.7 collective-permute-start.25
  163.8 15.1 %collective-permute-start.27 = (f32[32,4,1,128]{3,0,2,1:T(8,128)S(1)}, f32[32,4,1,128]{3,0,2,1:T(8,128)S(1)}, u32[]{:S(2)}, u32[]{:S(2)}) collective-permute-start(f32[32,4,1,128]{3,0,2,1:T(8,128)S(1)} %get-tuple-element.113), channel_id=1, source_target_pairs={{0,16},{16,32},{32,48},{1,17},{17,33},{33,49},{2,18},{18,34},{34,5... | collective-permute-start | bytes 196616 | tf_op jit(solution)/shard_map/ppermute | solution.py:20
  182.4 4.9 collective-permute-start.29
  189.0 6.5 collective-permute-start.30
  197.7 6.0 collective-permute-done.31
  203.7 15.1 %collective-permute-start.32 = (f32[32,4,1,128]{3,0,2,1:T(8,128)S(1)}, f32[32,4,1,128]{3,0,2,1:T(8,128)S(1)}, u32[]{:S(2)}, u32[]{:S(2)}) collective-permute-start(f32[32,4,1,128]{3,0,2,1:T(8,128)S(1)} %get-tuple-element.112), channel_id=1, source_target_pairs={{0,16},{16,32},{32,48},{1,17},{17,33},{33,49},{2,18},{18,34},{34,5... | collective-permute-start | bytes 196616 | tf_op jit(solution)/shard_map/ppermute | solution.py:20
  221.5 12.0 collective-permute-done.33
  234.1 6.0 collective-permute-start.34
  242.3 5.3 collective-permute-done.35
  247.8 212.4 %all-gather = f32[224,32,32]{2,1,0:T(8,128)S(1)} all-gather(f32[7,32,32]{2,1,0:T(8,128)S(1)} %fusion.2), channel_id=2, replica_groups=mesh['gx'=8,'gy'=4,'gz'=16] {'gx','gy'}, dimensions={0}, use_global_device_ids=true | all-gather | bytes 946176 | tf_op jit(solution)/shard_map/all_gather | solution.py:146
  460.7 50.5 %all_gather.7 = f32[112,32,32]{2,1,0:T(8,128)S(1)} all-gather(f32[7,32,32]{2,1,0:T(8,128)S(1)} %select_reduce_fusion), channel_id=1, replica_groups=mesh['gx'=8,'gy'=4,'gz'=16] {'gz'}, dimensions={0}, use_global_device_ids=true | all-gather | bytes 487424 | tf_op jit(solution)/shard_map/all_gather | solution.py:190
  511.2 4.3 broadcast_in_dim.82
  515.5 16.4 %scatter_fusion = f32[16,32,32,32]{3,1,2,0:T(8,128)} fusion(f32[16,32,32,32]{3,1,2,0:T(8,128)} %broadcast_in_dim.82, s32[112]{0:T(128)S(1)} %fusion.191, f32[112,32,32]{2,1,0:T(8,128)S(1)} %all_gather.7), kind=kCustom, calls=%fused_computation | custom fusion | flops 114688 | bytes 1377152 | tf_op jit(solution)/shard_map/scatter-add | solution.py:189
  531.9 9.0 copy.208
  540.9 6.2 reshape.408
  548.2 3.0 slice_select_fusion
  551.2 4.3 copy.210
  555.5 4.6 select_n.194
  560.1 101.7 %all-reduce.9.cloned.1.call-done = f32[512,256]{0,1:T(8,128)} async-done(((f32[512,256]{0,1:T(8,128)}), f32[512,256]{0,1:T(8,128)}) %all-reduce.9.cloned.1.call-update) | async-done | bytes 524304 | tf_op jit(solution)/shard_map/psum | solution.py:30
  664.6 214.9 %all-reduce.15.cloned.1.call-done = (f32[256,1024]{1,0:T(8,128)}, f32[256,256]{0,1:T(8,128)}) async-done(((f32[256,1024]{1,0:T(8,128)}, f32[256,256]{0,1:T(8,128)}), (f32[256,1024]{1,0:T(8,128)}, f32[256,256]{0,1:T(8,128)})) %all-reduce.15.cloned.1.call-update) | async-done | bytes 1310736 | tf_op jit(solution)/shard_map/psum | solution.py:30
  881.6 11.7 cholesky.130
  893.3 9.8 custom-call.19
  903.6 11.7 cholesky.147
  918.2 4.0 while.10
  922.2 19.8 %custom-call.20 = f32[2,128,128]{1,2,0:T(8,128)S(1)} custom-call(f32[2,128,128]{2,1,0:T(8,128)S(1)} %get-tuple-element.60), custom_call_target="InvertDiagBlocksLowerTriangular" | custom-call | tf_op jit(solution)/shard_map/jit(_solve_triangular)/triangular_solve | solution.py:212
  950.6 113.2 %all-reduce.11.cloned.1.call-done = f32[512,256]{0,1:T(8,128)} async-done(((f32[512,256]{0,1:T(8,128)}), f32[512,256]{0,1:T(8,128)}) %all-reduce.11.cloned.1.call-update) | async-done | bytes 524304 | tf_op jit(solution)/shard_map/psum | solution.py:30
  1066.4 214.9 %all-reduce.13.cloned.1.call-done = (f32[256,1024]{0,1:T(8,128)}, f32[256,256]{0,1:T(8,128)}) async-done(((f32[256,1024]{0,1:T(8,128)}, f32[256,256]{0,1:T(8,128)}), (f32[256,1024]{0,1:T(8,128)}, f32[256,256]{0,1:T(8,128)})) %all-reduce.13.cloned.1.call-update) | async-done | bytes 1310736 | tf_op jit(solution)/shard_map/psum | solution.py:30
  1283.5 11.7 cholesky.164
  1295.2 9.8 custom-call.22
  1305.5 11.7 cholesky.181
  1319.9 4.0 while.11
  1323.9 19.9 %custom-call.23 = f32[2,128,128]{1,2,0:T(8,128)S(1)} custom-call(f32[2,128,128]{2,1,0:T(8,128)S(1)} %get-tuple-element.62), custom_call_target="InvertDiagBlocksLowerTriangular" | custom-call | tf_op jit(solution)/shard_map/jit(_solve_triangular)/triangular_solve | solution.py:212
  1347.4 3.9 select_select_fusion
  1354.0 2.9 copy.215
  (240 shorter events, 94.8 us)
Async XLA Ops:
  6.5 655.2 %all-reduce.9.cloned.1.call-start = ((), (), s32[]{:S(2)}) async-start(), calls=%async_computation | async-start | bytes 1048576 | tf_op jit(solution)/shard_map/psum | solution.py:30
  7.3 16.5 %collective-permute-start = (f32[1,8,128]{2,1,0:T(8,128)S(1)}, f32[1,8,128]{2,1,0:T(8,128)S(1)}, u32[]{:S(2)}, u32[]{:S(2)}) collective-permute-start(f32[1,8,128]{2,1,0:T(8,128)S(1)} %get-tuple-element.146), channel_id=1, source_target_pairs={{64,0},{128,64},{192,128},{256,192},{320,256},{384,320},{448,384},... | collective-permute-start | bytes 12296 | tf_op jit(solution)/shard_map/ppermute | solution.py:23
  8.7 15.2 %collective-permute-start.1 = (f32[1,8,128]{2,1,0:T(8,128)S(1)}, f32[1,8,128]{2,1,0:T(8,128)S(1)}, u32[]{:S(2)}, u32[]{:S(2)}) collective-permute-start(f32[1,8,128]{2,1,0:T(8,128)S(1)} %get-tuple-element.145), channel_id=1, source_target_pairs={{0,64},{64,128},{128,192},{192,256},{256,320},{320,384},{384,448},... | collective-permute-start | bytes 12296 | tf_op jit(solution)/shard_map/ppermute | solution.py:20
  14.7 45.0 %collective-permute-start.7 = (f32[32,1,8,128]{3,0,2,1:T(8,128)S(1)}, f32[32,1,8,128]{3,0,2,1:T(8,128)S(1)}, u32[]{:S(2)}, u32[]{:S(2)}) collective-permute-start(f32[32,1,8,128]{3,0,2,1:T(8,128)S(1)} %get-tuple-element.130), channel_id=1, source_target_pairs={{0,64},{64,128},{128,192},{192,256},{256,320},{320,384},{384,448},... | collective-permute-start | bytes 393224 | tf_op jit(solution)/shard_map/ppermute | solution.py:20
  18.3 42.5 %collective-permute-start.6 = (f32[32,1,8,128]{3,0,2,1:T(8,128)S(1)}, f32[32,1,8,128]{3,0,2,1:T(8,128)S(1)}, u32[]{:S(2)}, u32[]{:S(2)}) collective-permute-start(f32[32,1,8,128]{3,0,2,1:T(8,128)S(1)} %get-tuple-element.129), channel_id=1, source_target_pairs={{64,0},{128,64},{192,128},{256,192},{320,256},{384,320},{448,384},... | collective-permute-start | bytes 393224 | tf_op jit(solution)/shard_map/ppermute | solution.py:23
  23.9 17.7 %collective-permute-start.3 = (f32[4,1,128]{2,1,0:T(1,128)S(1)}, f32[4,1,128]{2,1,0:T(1,128)S(1)}, u32[]{:S(2)}, u32[]{:S(2)}) collective-permute-start(f32[4,1,128]{2,1,0:T(1,128)S(1)} %get-tuple-element.143), channel_id=1, source_target_pairs={{0,16},{16,32},{32,48},{1,17},{17,33},{33,49},{2,18},{18,34},{34,5... | collective-permute-start | bytes 6152 | tf_op jit(solution)/shard_map/ppermute | solution.py:20
  39.7 13.6 collective-permute-start.2
  53.4 5.4 collective-permute-start.4
  54.7 4.9 collective-permute-start.5
  60.8 14.4 %collective-permute-start.8 = (f32[32,4,1,128]{3,0,2,1:T(8,128)S(1)}, f32[32,4,1,128]{3,0,2,1:T(8,128)S(1)}, u32[]{:S(2)}, u32[]{:S(2)}) collective-permute-start(f32[32,4,1,128]{3,0,2,1:T(8,128)S(1)} %get-tuple-element.120), channel_id=1, source_target_pairs={{16,0},{32,16},{48,32},{17,1},{33,17},{49,33},{18,2},{34,18},{50,3... | collective-permute-start | bytes 196616 | tf_op jit(solution)/shard_map/ppermute | solution.py:23
  62.7 13.8 %collective-permute-start.9 = (f32[32,4,1,128]{3,0,2,1:T(8,128)S(1)}, f32[32,4,1,128]{3,0,2,1:T(8,128)S(1)}, u32[]{:S(2)}, u32[]{:S(2)}) collective-permute-start(f32[32,4,1,128]{3,0,2,1:T(8,128)S(1)} %get-tuple-element.119), channel_id=1, source_target_pairs={{0,16},{16,32},{32,48},{1,17},{17,33},{33,49},{2,18},{18,34},{34,5... | collective-permute-start | bytes 196616 | tf_op jit(solution)/shard_map/ppermute | solution.py:20
  77.1 5.9 collective-permute-start.10
  78.7 5.2 collective-permute-start.11
  83.3 7.4 copy-start.7
  84.5 6.6 collective-permute-start.12
  85.8 6.8 collective-permute-start.13
  92.6 16.8 %collective-permute-start.14 = (f32[32,4,1,128]{3,0,2,1:T(8,128)S(1)}, f32[32,4,1,128]{3,0,2,1:T(8,128)S(1)}, u32[]{:S(2)}, u32[]{:S(2)}) collective-permute-start(f32[32,4,1,128]{3,0,2,1:T(8,128)S(1)} %get-tuple-element.118), channel_id=1, source_target_pairs={{16,0},{32,16},{48,32},{17,1},{33,17},{49,33},{18,2},{34,18},{50,3... | collective-permute-start | bytes 196616 | tf_op jit(solution)/shard_map/ppermute | solution.py:23
  94.5 16.3 %collective-permute-start.15 = (f32[32,4,1,128]{3,0,2,1:T(8,128)S(1)}, f32[32,4,1,128]{3,0,2,1:T(8,128)S(1)}, u32[]{:S(2)}, u32[]{:S(2)}) collective-permute-start(f32[32,4,1,128]{3,0,2,1:T(8,128)S(1)} %get-tuple-element.117), channel_id=1, source_target_pairs={{0,16},{16,32},{32,48},{1,17},{17,33},{33,49},{2,18},{18,34},{34,5... | collective-permute-start | bytes 196616 | tf_op jit(solution)/shard_map/ppermute | solution.py:20
  110.9 8.5 copy-start.2
  111.5 7.3 collective-permute-start.16
  113.1 6.0 collective-permute-start.17
  119.8 6.7 collective-permute-start.18
  121.1 6.9 collective-permute-start.19
  128.1 16.8 %collective-permute-start.20 = (f32[32,4,1,128]{3,0,2,1:T(8,128)S(1)}, f32[32,4,1,128]{3,0,2,1:T(8,128)S(1)}, u32[]{:S(2)}, u32[]{:S(2)}) collective-permute-start(f32[32,4,1,128]{3,0,2,1:T(8,128)S(1)} %get-tuple-element.116), channel_id=1, source_target_pairs={{16,0},{32,16},{48,32},{17,1},{33,17},{49,33},{18,2},{34,18},{50,3... | collective-permute-start | bytes 196616 | tf_op jit(solution)/shard_map/ppermute | solution.py:23
  130.0 15.6 %collective-permute-start.21 = (f32[32,4,1,128]{3,0,2,1:T(8,128)S(1)}, f32[32,4,1,128]{3,0,2,1:T(8,128)S(1)}, u32[]{:S(2)}, u32[]{:S(2)}) collective-permute-start(f32[32,4,1,128]{3,0,2,1:T(8,128)S(1)} %get-tuple-element.115), channel_id=1, source_target_pairs={{0,16},{16,32},{32,48},{1,17},{17,33},{33,49},{2,18},{18,34},{34,5... | collective-permute-start | bytes 196616 | tf_op jit(solution)/shard_map/ppermute | solution.py:20
  146.1 6.2 collective-permute-start.22
  147.7 5.4 collective-permute-start.23
  153.9 6.5 collective-permute-start.24
  155.2 6.7 collective-permute-start.25
  161.9 17.2 %collective-permute-start.26 = (f32[32,4,1,128]{3,0,2,1:T(8,128)S(1)}, f32[32,4,1,128]{3,0,2,1:T(8,128)S(1)}, u32[]{:S(2)}, u32[]{:S(2)}) collective-permute-start(f32[32,4,1,128]{3,0,2,1:T(8,128)S(1)} %get-tuple-element.114), channel_id=1, source_target_pairs={{16,0},{32,16},{48,32},{17,1},{33,17},{49,33},{18,2},{34,18},{50,3... | collective-permute-start | bytes 196616 | tf_op jit(solution)/shard_map/ppermute | solution.py:23
  163.8 16.4 %collective-permute-start.27 = (f32[32,4,1,128]{3,0,2,1:T(8,128)S(1)}, f32[32,4,1,128]{3,0,2,1:T(8,128)S(1)}, u32[]{:S(2)}, u32[]{:S(2)}) collective-permute-start(f32[32,4,1,128]{3,0,2,1:T(8,128)S(1)} %get-tuple-element.113), channel_id=1, source_target_pairs={{0,16},{16,32},{32,48},{1,17},{17,33},{33,49},{2,18},{18,34},{34,5... | collective-permute-start | bytes 196616 | tf_op jit(solution)/shard_map/ppermute | solution.py:20
  180.8 6.7 collective-permute-start.28
  182.4 5.8 collective-permute-start.29
  189.0 8.7 collective-permute-start.30
  195.5 8.2 collective-permute-start.31
  203.7 17.8 %collective-permute-start.32 = (f32[32,4,1,128]{3,0,2,1:T(8,128)S(1)}, f32[32,4,1,128]{3,0,2,1:T(8,128)S(1)}, u32[]{:S(2)}, u32[]{:S(2)}) collective-permute-start(f32[32,4,1,128]{3,0,2,1:T(8,128)S(1)} %get-tuple-element.112), channel_id=1, source_target_pairs={{0,16},{16,32},{32,48},{1,17},{17,33},{33,49},{2,18},{18,34},{34,5... | collective-permute-start | bytes 196616 | tf_op jit(solution)/shard_map/ppermute | solution.py:20
  218.8 14.7 %collective-permute-start.33 = (f32[32,4,1,128]{3,0,2,1:T(8,128)S(1)}, f32[32,4,1,128]{3,0,2,1:T(8,128)S(1)}, u32[]{:S(2)}, u32[]{:S(2)}) collective-permute-start(f32[32,4,1,128]{3,0,2,1:T(8,128)S(1)} %get-tuple-element.111), channel_id=1, source_target_pairs={{16,0},{32,16},{48,32},{17,1},{33,17},{49,33},{18,2},{34,18},{50,3... | collective-permute-start | bytes 196616 | tf_op jit(solution)/shard_map/ppermute | solution.py:23
  234.1 8.0 collective-permute-start.34
  240.4 7.2 collective-permute-start.35
  547.2 4.0 copy-start
  548.1 331.4 %all-reduce.15.cloned.1.call-start = ((), (), s32[]{:S(2)}) async-start(), calls=%async_computation.3 | async-start | bytes 2621440 | tf_op jit(solution)/shard_map/psum | solution.py:30
  663.5 278.6 %copy-start.3 = (f32[512,256]{0,1:T(8,128)S(1)}, f32[512,256]{0,1:T(8,128)}, u32[]{:S(2)}) copy-start(f32[512,256]{0,1:T(8,128)} %all-reduce.9.cloned.1.call-done) | copy-start | bytes 1572868
  663.5 400.4 %all-reduce.11.cloned.1.call-start = ((), (), s32[]{:S(2)}) async-start(), calls=%async_computation.1 | async-start | bytes 1048576 | tf_op jit(solution)/shard_map/psum | solution.py:30
  903.2 40.1 %copy-start.5 = (f32[256,1024]{1,0:T(8,128)S(1)}, f32[256,1024]{1,0:T(8,128)}, u32[]{:S(2)}) copy-start(f32[256,1024]{1,0:T(8,128)} %get-tuple-element.84) | copy-start | bytes 3145732
  942.8 2.3 copy-start.1
  949.5 331.9 %all-reduce.13.cloned.1.call-start = ((), (), s32[]{:S(2)}) async-start(), calls=%async_computation.2 | async-start | bytes 2621440 | tf_op jit(solution)/shard_map/psum | solution.py:30
  1065.5 278.4 %copy-start.4 = (f32[512,256]{0,1:T(8,128)S(1)}, f32[512,256]{0,1:T(8,128)}, u32[]{:S(2)}) copy-start(f32[512,256]{0,1:T(8,128)} %all-reduce.11.cloned.1.call-done) | copy-start | bytes 1572868
  1343.9 1.3 copy-start.6
Sparse Core Ops, SparseCore 0:
  548.2 113.5 all-reduce.8
  664.2 215.2 all-reduce.14
  949.6 114.1 all-reduce.10
  1066.1 215.2 all-reduce.12
where the time goes:
time: 1370 us; the launch traced here: 1360 us
  waiting for transfers between devices  692 us (51%)
  blocking collectives  263 us (19%)
  starting transfers between devices  173 us (13%)
  other arithmetic  151 us (11%)
  local copies, waits for them, and re-layouts  51.9 us (4%)
  between operations  17.3 us (1%)
  matrix products  15.8 us (1%)
    psum x4, waiting for transfers between devices, from_root(): return lax.psum(kept, axis)  645 us
    all_gather x1, blocking collectives, on_device(): piece = lax.all_gather(blocks[None], ('gx', 'gy'), axis=0, tiled=True)  212 us
    ppermute x18, starting transfers between devices, with_halo(): lax.ppermute(lax.slice_in_dim(block, block.shape[dim] - width, None, axis...  145 us
    another operation x14, other arithmetic, on_device(): factor = jnp.linalg.cholesky(diagonal_piece)  69.3 us
    all_gather x1, blocking collectives, on_device(): lax.all_gather(owned, 'gz', axis=0, tiled=True)  50.5 us
    another operation x5, other arithmetic, on_device(): jax.scipy.linalg.solve_triangular(factor, column_piece.T, lower=True)  39.8 us
    ppermute x18, waiting for transfers between devices, with_halo(): lax.ppermute(lax.slice_in_dim(block, 0, width, axis=dim), axis, backward)  36 us
  transfers between devices with their start and end apart: 40, of which 24 were waited for; matrix products, arithmetic and copies ran while one was open for 2% of the time, Pallas kernels for 0%

commit v1 on v0

--- a/solution.py
+++ b/solution.py
@@ -27,7 +27,7 @@
 
 def from_root(value, axis, source):
     kept = jnp.where(lax.axis_index(axis) == source, value, 0).astype(value.dtype)
-    return lax.psum(kept, axis)
+    return jnp.sum(lax.all_gather(kept, axis), axis=0)
 
 
 def cheb_factors(step_index):

time: 1370 us -> 5790 us (4.23)
  waiting for transfers between devices: 692 us -> 5010 us
    all_gather x0 -> x6, waiting for transfers between devices: none -> 4960 us  [from_root(): return jnp.sum(lax.all_gather(kept, axis), axis=0)]
    psum x4 -> x0, waiting for transfers between devices: 645 us -> none  [from_root(): return lax.psum(kept, axis)]
  transfers between devices with their start and end apart: 40 -> 42, of which waited for: 24 -> 25; matrix products, arithmetic and copies ran while one was open for 2% -> 3% of each run, Pallas kernels for 0% -> 0%
where the time goes in v1:
time: 5790 us; the launch traced here: 5750 us
  waiting for transfers between devices  5010 us (87%)
  blocking collectives  256 us (4%)
  other arithmetic  180 us (3%)
  starting transfers between devices  167 us (3%)
  local copies, waits for them, and re-layouts  108 us (2%)
    all_gather x6, waiting for transfers between devices, from_root(): return jnp.sum(lax.all_gather(kept, axis), axis=0)  4960 us
    all_gather x1, blocking collectives, on_device(): piece = lax.all_gather(blocks[None], ('gx', 'gy'), axis=0, tiled=True)  235 us
    ppermute x18, starting transfers between devices, with_halo(): lax.ppermute(lax.slice_in_dim(block, block.shape[dim] - width, None, axis...  135 us
  transfers between devices with their start and end apart: 42, of which 25 were waited for; matrix products, arithmetic and copies ran while one was open for 3% of the time, Pallas kernels for 0%

profile of v1, /device:TPU:1, one launch (start us, length us, event | category | flops | bytes accessed | tf_op | source)
XLA Modules:
  0.0 5752.1 jit_solution(17542368732654720280)
XLA Ops:
  7.6 4.4 collective-permute-start.7
  15.4 4.8 collective-permute-start.1
  24.6 6.1 collective-permute-start.2
  30.6 11.6 collective-permute-start.3
  53.8 14.3 collective-permute-start.9
  80.1 4.3 collective-permute-start.13
  88.2 15.5 collective-permute-start.15
  107.0 4.4 collective-permute-start.17
  118.6 4.0 collective-permute-start.19
  126.5 15.6 collective-permute-start.21
  156.2 4.0 collective-permute-start.25
  164.1 15.5 collective-permute-start.27
  191.1 4.1 collective-permute-start.30
  197.3 4.5 collective-permute-done.31
  201.8 15.2 collective-permute-start.32
  219.7 12.4 collective-permute-done.33
  241.8 234.9 %all-gather = f32[224,32,32]{2,1,0:T(8,128)S(1)} all-gather(f32[7,32,32]{2,1,0:T(8,128)S(1)} %fusion.2), channel_id=2, replica_groups=mesh['gx'=8,'gy'=4,'gz'=16] {'gx','gy'}, dimensions={0}, use_global_device_ids=true | all-gather | bytes 946176 | tf_op jit(solution)/shard_map/all_gather | solution.py:146
  477.2 21.6 all_gather.41
  498.8 4.3 broadcast_in_dim.82
  503.1 19.3 scatter_fusion
  522.5 9.0 copy.208
  531.5 6.2 reshape.418
  538.7 84.4 %all-gather.15.cloned.1.call-done = f32[8192,256]{0,1:T(8,128)} async-done(((f32[512,256]{0,1:T(8,128)}), f32[8192,256]{0,1:T(8,128)}) %all-gather.15.cloned.1.call-update) | async-done | bytes 8388624 | tf_op jit(solution)/shard_map/all_gather | solution.py:30
  623.1 10.9 copy.224
  641.3 4.3 copy.210
  645.7 4.6 select_n.201
  651.0 509.4 %all-gather.17.cloned.1.call-done = f32[8192,256]{0,1:T(8,128)} async-done(((f32[256,256]{0,1:T(8,128)}), f32[8192,256]{0,1:T(8,128)}) %all-gather.17.cloned.1.call-update) | async-done | bytes 8388624 | tf_op jit(solution)/shard_map/all_gather | solution.py:30
  1160.4 6.8 copy.225
  1169.6 11.7 cholesky.130
  1181.3 9.8 custom-call.19
  1191.6 11.7 cholesky.147
  1206.1 3.9 while.10
  1209.9 19.9 custom-call.20
  1231.1 1887.9 %all-gather.13.cloned.1.call-done = f32[32,256,1024]{2,1,0:T(8,128)} async-done(((f32[1,256,1024]{2,1,0:T(8,128)}), f32[32,256,1024]{2,1,0:T(8,128)}) %all-gather.13.cloned.1.call-update) | async-done | bytes 33554448 | tf_op jit(solution)/shard_map/all_gather | solution.py:30
  3119.0 11.8 reduce_sum.119
  3137.5 87.9 %all-gather.19.cloned.1.call-done = f32[8192,256]{0,1:T(8,128)} async-done(((f32[512,256]{0,1:T(8,128)}), f32[8192,256]{0,1:T(8,128)}) %all-gather.19.cloned.1.call-update) | async-done | bytes 8388624 | tf_op jit(solution)/shard_map/all_gather | solution.py:30
  3225.4 10.9 copy.226
  3242.6 520.1 %all-gather.21.cloned.1.call-done = f32[8192,256]{0,1:T(8,128)} async-done(((f32[256,256]{0,1:T(8,128)}), f32[8192,256]{0,1:T(8,128)}) %all-gather.21.cloned.1.call-update) | async-done | bytes 8388624 | tf_op jit(solution)/shard_map/all_gather | solution.py:30
  3762.7 6.8 copy.227
  3771.9 11.7 cholesky.164
  3783.6 9.8 custom-call.22
  3793.9 11.7 cholesky.181
  3808.2 3.8 while.11
  3812.0 19.9 custom-call.23
  3833.1 1868.7 %all-gather.23.cloned.1.call-done = f32[8192,1024]{0,1:T(8,128)} async-done(((f32[256,1024]{0,1:T(8,128)}), f32[8192,1024]{0,1:T(8,128)}) %all-gather.23.cloned.1.call-update) | async-done | bytes 33554448 | tf_op jit(solution)/shard_map/all_gather | solution.py:30
  5701.8 19.6 copy.228
  5721.4 7.7 bitcast_reduce_fusion
  5734.9 4.6 select_select_fusion
  (251 shorter events, 145.6 us)
Async XLA Ops:
  6.5 616.6 %all-gather.15.cloned.1.call-start = ((), (), s32[]{:S(2)}) async-start(), calls=%async_computation.1 | async-start | bytes 8912896 | tf_op jit(solution)/shard_map/all_gather | solution.py:30
  7.6 43.2 collective-permute-start.7
  12.0 39.9 collective-permute-start.6
  14.1 10.4 collective-permute-start
  15.4 9.1 collective-permute-start.1
  24.6 17.7 collective-permute-start.2
  30.6 12.3 collective-permute-start.3
  43.0 4.5 collective-permute-start.5
  46.2 4.5 collective-permute-start.4
  51.9 16.4 collective-permute-start.8
  53.8 15.6 collective-permute-start.9
  69.8 14.6 copy-start.3
  70.1 4.7 collective-permute-start.11
  73.5 4.5 collective-permute-start.10
  78.8 6.1 collective-permute-start.12
  80.1 6.2 collective-permute-start.13
  84.8 32.0 copy-start.2
  86.3 17.4 collective-permute-start.14
  88.2 18.2 collective-permute-start.15
  107.0 7.2 collective-permute-start.17
  111.7 4.8 collective-permute-start.16
  117.3 5.7 collective-permute-start.18
  118.6 5.9 collective-permute-start.19
  124.6 18.2 collective-permute-start.20
  126.5 18.2 collective-permute-start.21
  145.3 5.4 collective-permute-start.23
  149.3 4.8 collective-permute-start.22
  154.9 5.7 collective-permute-start.24
  156.2 5.9 collective-permute-start.25
  162.1 17.5 collective-permute-start.26
  164.1 16.8 collective-permute-start.27
  181.5 5.5 collective-permute-start.29
  185.5 4.8 collective-permute-start.28
  191.1 6.2 collective-permute-start.30
  195.2 6.6 collective-permute-start.31
  201.8 17.9 collective-permute-start.32
  217.1 15.0 collective-permute-start.33
  232.7 5.7 collective-permute-start.34
  236.7 4.8 collective-permute-start.35
  537.8 96.3 %copy-start = (f32[512,1024]{0,1:T(8,128)}, f32[512,1024]{0,1:T(8,128)S(1)}, u32[]{:S(2)}) copy-start(f32[512,1024]{0,1:T(8,128)S(1)} %reshape.418) | copy-start | bytes 6291460
  538.7 621.8 %all-gather.17.cloned.1.call-start = ((), (), s32[]{:S(2)}) async-start(), calls=%async_computation.2 | async-start | bytes 8650752 | tf_op jit(solution)/shard_map/all_gather | solution.py:30
  637.9 2481.1 %all-gather.13.cloned.1.call-start = ((), (), s32[]{:S(2)}) async-start(), calls=%async_computation | async-start | bytes 34603008 | tf_op jit(solution)/shard_map/all_gather | solution.py:30
  650.3 2575.1 %all-gather.19.cloned.1.call-start = ((), (), s32[]{:S(2)}) async-start(), calls=%async_computation.3 | async-start | bytes 8912896 | tf_op jit(solution)/shard_map/all_gather | solution.py:30
  3130.9 1.9 copy-start.1
  3137.0 625.7 %all-gather.21.cloned.1.call-start = ((), (), s32[]{:S(2)}) async-start(), calls=%async_computation.4 | async-start | bytes 8650752 | tf_op jit(solution)/shard_map/all_gather | solution.py:30
  3240.2 2461.6 %all-gather.23.cloned.1.call-start = ((), (), s32[]{:S(2)}) async-start(), calls=%async_computation.5 | async-start | bytes 34603008 | tf_op jit(solution)/shard_map/all_gather | solution.py:30
Sparse Core Ops, SparseCore 0:
  538.8 84.2 all-gather.14
  638.0 522.4 all-gather.16
  1162.5 1956.4 all-gather.12
  3137.1 88.2 all-gather.18
  3240.3 522.4 all-gather.20
  3764.7 1937.0 all-gather.22
